TPU v7x, 32 devices: a whole 2x2x4 slice. The times are simulated.
32 devices in a mesh: fields: 2 (over x), seq: 8 (over z, y), head: 2 (over core).
Axes of the slice: x: 2, y: 2, z: 4, core: 2. Of those that a mesh axis runs over, the one named last changes fastest.
Arguments:
- tokens: bfloat16 [65536, 512], P(('fields', 'seq')), parts along dimension 0, may hold values from -6 to 6
- norm_gain: float32 [512], replicated, may hold values from 0.1 to 1.9
- coarse_gain: float32 [512], replicated, may hold values from 0.25 to 2.5
- w_query: bfloat16 [512, 512], P(None, 'head'), may hold values from -0.25 to 0.25
- w_key: bfloat16 [512, 512], P(None, 'head'), may hold values from -0.25 to 0.25
- w_value: bfloat16 [512, 512], P(None, 'head'), may hold values from -0.25 to 0.25
- w_out: bfloat16 [512, 512], replicated, may hold values from -0.25 to 0.25
- score_scale: float32 [8], P('head'), may hold values from 1 to 40, as said below
Outputs:
- attn_out: bfloat16 [65536, 512], P(('fields', 'seq'), 'head'), parts along dimension 0
There are 2 independent parts, one for each index of `fields`. A program takes and returns all parts, laid end to end along the dimension named above; an argument that names none is the same for every part. Nothing has to cross between parts.
Inputs may be any that keep to these rules, and one draw needn't show every extreme that they name: `score_scale`: per-head score temperature.
All inputs are finite; a program needn't handle non-finite values.
Results may differ from a plain program's by a relative error of at most 0.0035.
The roundings to bfloat16 on the way count: a program that leaves them out, or rounds other values in their place, can miss the bound.
Values may be sent and summed in bfloat16 or wider, within the bound.
No kernel may reach another device: no remote copies, remote signals or barrier semaphores. Data moves between devices by JAX's collectives and lax.ppermute only.
A program may use at most 64 MiB of HBM per device.

v0:
```python
import jax
import jax.numpy as jnp
from jax import lax
from jax.sharding import PartitionSpec as P

HEAD_DIM = 64
WINDOW = 256
POOL = 1024
QB = 512


def with_halo(block, sides, width):
    for axis, dim in sides:
        count = lax.axis_size(axis)
        forward = [(i, i + 1) for i in range(count - 1)]
        backward = [(target, source) for source, target in forward]
        low = lax.ppermute(
            lax.slice_in_dim(block, block.shape[dim] - width, None, axis=dim), axis, forward
        )
        high = lax.ppermute(lax.slice_in_dim(block, 0, width, axis=dim), axis, backward)
        block = jnp.concatenate([low, block, high], axis=dim)
    return block


def rms_rows(matrix, scaling):
    return matrix * lax.rsqrt(jnp.mean(matrix * matrix, axis=-1, keepdims=True) + 1e-05) * scaling


def unit_heads(matrix, head_count):
    split = matrix.reshape(matrix.shape[0], head_count, HEAD_DIM)
    return split * lax.rsqrt(jnp.mean(split * split, axis=-1, keepdims=True) + 1e-06)


def body(tokens, norm_gain, coarse_gain, w_query, w_key, w_value, w_out, score_scale):
    tok_count = tokens.shape[0]
    full_width = tokens.shape[1]
    local_heads = score_scale.shape[0]
    width = local_heads * HEAD_DIM
    seq_index = lax.axis_index("seq")
    total_tokens = tok_count * lax.axis_size("seq")
    normed = rms_rows(tokens.astype(jnp.float32), norm_gain).astype(jnp.bfloat16)
    factor = (score_scale * HEAD_DIM ** (-0.5))[None, :, None]
    queries = (
        unit_heads(jnp.dot(normed, w_query, preferred_element_type=jnp.float32), local_heads)
        * factor
    ).astype(jnp.bfloat16)
    key_rows = unit_heads(
        jnp.dot(normed, w_key, preferred_element_type=jnp.float32), local_heads
    ).astype(jnp.bfloat16)
    value_rows = jnp.dot(normed, w_value, preferred_element_type=jnp.float32).astype(jnp.bfloat16)
    stacked = jnp.stack([key_rows.reshape(tok_count, width), value_rows])
    extended = with_halo(stacked, (("seq", 1),), WINDOW)
    extended = extended.reshape(2, tok_count + 2 * WINDOW, local_heads, HEAD_DIM)
    normed_kept = lax.optimization_barrier(normed)
    pooled = jnp.mean(
        normed_kept.astype(jnp.float32).reshape(tok_count // POOL, POOL, full_width), axis=1
    )
    coarse = rms_rows(pooled, coarse_gain).astype(jnp.bfloat16)
    coarse_keys = unit_heads(
        jnp.dot(coarse, w_key, preferred_element_type=jnp.float32), local_heads
    ).astype(jnp.bfloat16)
    coarse_values = jnp.dot(coarse, w_value, preferred_element_type=jnp.float32).astype(
        jnp.bfloat16
    )
    coarse_stack = jnp.stack([coarse_keys.reshape(coarse.shape[0], width), coarse_values])
    coarse_all = lax.all_gather(coarse_stack, "seq", axis=1, tiled=True)
    coarse_all = coarse_all.reshape(2, coarse_all.shape[1], local_heads, HEAD_DIM)
    span = QB + 2 * WINDOW
    offsets = (
        jnp.arange(QB, dtype=jnp.int32)[:, None]
        - jnp.arange(span, dtype=jnp.int32)[None, :]
        + WINDOW
    )
    near = jnp.abs(offsets) <= WINDOW

    def one_block(block_id):
        row_start = block_id * QB
        block_queries = lax.dynamic_slice_in_dim(queries, row_start, QB, 0)
        block_keys = lax.dynamic_slice_in_dim(extended[0], row_start, span, 0)
        block_values = lax.dynamic_slice_in_dim(extended[1], row_start, span, 0)
        band = jnp.einsum(
            "qhd,khd->hqk", block_queries, block_keys, preferred_element_type=jnp.float32
        )
        positions = seq_index * tok_count + row_start + jnp.arange(span, dtype=jnp.int32) - WINDOW
        inside = (positions >= 0) & (positions < total_tokens)
        band = jnp.where(near[None] & inside[None, None, :], band, -1e30)
        far = jnp.einsum(
            "qhd,khd->hqk", block_queries, coarse_all[0], preferred_element_type=jnp.float32
        )
        peak = jnp.maximum(
            jnp.max(band, axis=-1, keepdims=True), jnp.max(far, axis=-1, keepdims=True)
        )
        band_exp = jnp.exp(band - peak)
        far_exp = jnp.exp(far - peak)
        total = jnp.sum(band_exp, axis=-1, keepdims=True) + jnp.sum(far_exp, axis=-1, keepdims=True)
        band_weights = (band_exp / total).astype(jnp.bfloat16)
        far_weights = (far_exp / total).astype(jnp.bfloat16)
        mixed = jnp.einsum(
            "hqk,khd->qhd", band_weights, block_values, preferred_element_type=jnp.float32
        )
        mixed = mixed + jnp.einsum(
            "hqk,khd->qhd", far_weights, coarse_all[1], preferred_element_type=jnp.float32
        )
        return mixed.astype(jnp.bfloat16).reshape(QB, width)

    attended = lax.map(one_block, jnp.arange(tok_count // QB, dtype=jnp.int32)).reshape(
        tok_count, width
    )
    head_index = lax.axis_index("head")
    own_rows = lax.dynamic_slice_in_dim(w_out, head_index * width, width, 0)
    partial_out = jnp.dot(attended, own_rows, preferred_element_type=jnp.float32)
    summed = lax.psum_scatter(partial_out, "head", scatter_dimension=1, tiled=True)
    return summed.astype(jnp.bfloat16)


def solution(mesh):
    return jax.shard_map(
        body,
        mesh=mesh,
        in_specs=(
            P(("fields", "seq"), None),
            P(),
            P(),
            P(None, "head"),
            P(None, "head"),
            P(None, "head"),
            P(),
            P("head"),
        ),
        out_specs=P(("fields", "seq"), "head"),
        check_vma=False,
    )
```

profile of v0, /device:TPU:0, one launch (start us, length us, event | category | flops | bytes accessed | tf_op | source)
XLA Modules:
  0.0 215.3 jit_solution(245271120795114434)
XLA Ops:
  6.5 3.2 %fusion.30 = f32[4096]{0:T(1024)S(1)} fusion(bf16[4096,512]{1,0:T(8,128)(2,1)} %param.10), kind=kLoop, calls=%fused_computation.40 | loop fusion | flops 6287360 | bytes 4210688 | tf_op jit(solution)/shard_map/reduce_sum | solution.py:26
  15.5 4.9 %collective-permute-start = (bf16[2,256,256]{1,2,0:T(8,128)(2,1)}, bf16[2,256,256]{1,2,0:T(8,128)(2,1)S(1)}, u32[]{:S(2)}, u32[]{:S(2)}) collective-permute-start(bf16[2,256,256]{1,2,0:T(8,128)(2,1)} %get-tuple-element.173), channel_id=1, source_target_pairs={{0,2},{2,4},{4,6},{6,8},{8,10},{10,12},{12,14},{1,3},{3,5},{5,7},{... | collective-permute-start | bytes 786440 | tf_op jit(solution)/shard_map/ppermute | solution.py:17
  22.9 3.6 %multiply_reduce_fusion = (f32[4096,4]{0,1:T(4,128)S(1)}, f32[4096,256]{0,1:T(8,128)S(1)}) fusion(bf16[4096,512]{1,0:T(8,128)(2,1)} %copy-done.1, bf16[512,256]{1,0:T(8,128)(2,1)S(1)} %copy-done.5), kind=kOutput, calls=%fused_computation.51 | convolution fusion | flops 1075822592 | bytes 8716288 | tf_op jit(solution)/shard_map/dot_general | solution.py:44
  29.6 32.9 %all_gather.3 = bf16[2,32,256]{2,0,1:T(2,128)(2,1)S(1)} all-gather(bf16[2,4,256]{2,0,1:T(2,128)(2,1)S(1)} %copy.19), channel_id=1, replica_groups=mesh['fields'=2,'seq'=8,'head'=2] {'seq'}, dimensions={1}, use_global_device_ids=true | all-gather | bytes 36864 | tf_op jit(solution)/shard_map/all_gather | solution.py:66
  62.7 3.6 %pad_maximum_fusion = bf16[2,4608,256]{1,2,0:T(8,128)(2,1)} fusion(bf16[2,256,256]{1,2,0:T(8,128)(2,1)} %collective-permute-done.1, bf16[1,4096,256]{1,2,0:T(8,128)(2,1)} %copy-done.3, bf16[1,4096,256]{1,2,0:T(8,128)(2,1)S(1)} %bitcast.76, bf16[2,256,256]{1,2,0:T(8,128)(2,1)S(1)} %collective-permute-done), kind=kLoop, calls=%fused_computation.46 | loop fusion | flops 18874368 | bytes 9437184 | tf_op jit(solution)/shard_map/concatenate | solution.py:21
  66.4 114.6 %while.13 = (s32[]{:T(128)}, bf16[8,512,256]{2,1,0:T(8,128)(2,1)}, bf16[2,4608,4,64]{1,3,2,0:T(8,128)(2,1)}, s32[8]{0:T(128)S(1)}, s32[]{:T(128)}, /*index=5*/bf...) while((s32[]{:T(128)}, bf16[8,512,256]{2,1,0:T(8,128)(2,1)}, ...), condition=%wide.region_11.12_spmd.clone, body=%wide.region_6.11_spmd.clone.sunk | while | flops 575800320 | bytes 41618152 | solution.py:106
  68.2 2.8 %fusion.67 = (bf16[1,4608,4,64]{1,3,2,0:T(8,128)(2,1)S(1)}, bf16[1,4608,4,64]{1,3,2,0:T(8,128)(2,1)S(1)}) fusion(bf16[2,4608,4,64]{1,3,2,0:T(8,128)(2,1)} %get-tuple-element.262), kind=kLoop, calls=%fused_computation.71.clone.1 | loop fusion | bytes 9437184 | tf_op jit(solution)/shard_map/while/body/eval_jaxpr/slice | solution.py:80
  77.0 2.5 %fusion.71 = f32[512,4,64]{0,2,1:T(8,128)S(1)} fusion(f32[4,512,1024]{2,1,0:T(8,128)S(1)} %get-tuple-element.231, f32[4,512]{1,0:T(4,128)S(1)} %add.173, f32[4,512]{1,0:T(4,128)S(1)} %max.13, pred[512,1024]{1,0:T(8,128)(4,1)S(1)} %fusion.66, bf16[1,4608,4,64]{1,3,2,0:T(8,128)(2,1)S(1)} %get-tuple-element.235, s32[]{:T(128)S(6)} %select_n.44), kind=kOutput, calls=%fused_computation.8.clone.1 | convolution fusion | flops 276824064 | bytes 9977860 | tf_op jit(solution)/shard_map/while/body/eval_jaxpr/hqk,khd->qhd/dot_general | solution.py:98
  82.5 2.8 %fusion.67 = (bf16[1,4608,4,64]{1,3,2,0:T(8,128)(2,1)S(1)}, bf16[1,4608,4,64]{1,3,2,0:T(8,128)(2,1)S(1)}) fusion(bf16[2,4608,4,64]{1,3,2,0:T(8,128)(2,1)} %get-tuple-element.262), kind=kLoop, calls=%fused_computation.71.clone.1 | loop fusion | bytes 9437184 | tf_op jit(solution)/shard_map/while/body/eval_jaxpr/slice | solution.py:80
  91.4 2.5 %fusion.71 = f32[512,4,64]{0,2,1:T(8,128)S(1)} fusion(f32[4,512,1024]{2,1,0:T(8,128)S(1)} %get-tuple-element.231, f32[4,512]{1,0:T(4,128)S(1)} %add.173, f32[4,512]{1,0:T(4,128)S(1)} %max.13, pred[512,1024]{1,0:T(8,128)(4,1)S(1)} %fusion.66, bf16[1,4608,4,64]{1,3,2,0:T(8,128)(2,1)S(1)} %get-tuple-element.235, s32[]{:T(128)S(6)} %select_n.44), kind=kOutput, calls=%fused_computation.8.clone.1 | convolution fusion | flops 276824064 | bytes 9977860 | tf_op jit(solution)/shard_map/while/body/eval_jaxpr/hqk,khd->qhd/dot_general | solution.py:98
  96.9 2.8 %fusion.67 = (bf16[1,4608,4,64]{1,3,2,0:T(8,128)(2,1)S(1)}, bf16[1,4608,4,64]{1,3,2,0:T(8,128)(2,1)S(1)}) fusion(bf16[2,4608,4,64]{1,3,2,0:T(8,128)(2,1)} %get-tuple-element.262), kind=kLoop, calls=%fused_computation.71.clone.1 | loop fusion | bytes 9437184 | tf_op jit(solution)/shard_map/while/body/eval_jaxpr/slice | solution.py:80
  105.7 2.5 %fusion.71 = f32[512,4,64]{0,2,1:T(8,128)S(1)} fusion(f32[4,512,1024]{2,1,0:T(8,128)S(1)} %get-tuple-element.231, f32[4,512]{1,0:T(4,128)S(1)} %add.173, f32[4,512]{1,0:T(4,128)S(1)} %max.13, pred[512,1024]{1,0:T(8,128)(4,1)S(1)} %fusion.66, bf16[1,4608,4,64]{1,3,2,0:T(8,128)(2,1)S(1)} %get-tuple-element.235, s32[]{:T(128)S(6)} %select_n.44), kind=kOutput, calls=%fused_computation.8.clone.1 | convolution fusion | flops 276824064 | bytes 9977860 | tf_op jit(solution)/shard_map/while/body/eval_jaxpr/hqk,khd->qhd/dot_general | solution.py:98
  111.2 2.8 %fusion.67 = (bf16[1,4608,4,64]{1,3,2,0:T(8,128)(2,1)S(1)}, bf16[1,4608,4,64]{1,3,2,0:T(8,128)(2,1)S(1)}) fusion(bf16[2,4608,4,64]{1,3,2,0:T(8,128)(2,1)} %get-tuple-element.262), kind=kLoop, calls=%fused_computation.71.clone.1 | loop fusion | bytes 9437184 | tf_op jit(solution)/shard_map/while/body/eval_jaxpr/slice | solution.py:80
  120.0 2.5 %fusion.71 = f32[512,4,64]{0,2,1:T(8,128)S(1)} fusion(f32[4,512,1024]{2,1,0:T(8,128)S(1)} %get-tuple-element.231, f32[4,512]{1,0:T(4,128)S(1)} %add.173, f32[4,512]{1,0:T(4,128)S(1)} %max.13, pred[512,1024]{1,0:T(8,128)(4,1)S(1)} %fusion.66, bf16[1,4608,4,64]{1,3,2,0:T(8,128)(2,1)S(1)} %get-tuple-element.235, s32[]{:T(128)S(6)} %select_n.44), kind=kOutput, calls=%fused_computation.8.clone.1 | convolution fusion | flops 276824064 | bytes 9977860 | tf_op jit(solution)/shard_map/while/body/eval_jaxpr/hqk,khd->qhd/dot_general | solution.py:98
  125.5 2.8 %fusion.67 = (bf16[1,4608,4,64]{1,3,2,0:T(8,128)(2,1)S(1)}, bf16[1,4608,4,64]{1,3,2,0:T(8,128)(2,1)S(1)}) fusion(bf16[2,4608,4,64]{1,3,2,0:T(8,128)(2,1)} %get-tuple-element.262), kind=kLoop, calls=%fused_computation.71.clone.1 | loop fusion | bytes 9437184 | tf_op jit(solution)/shard_map/while/body/eval_jaxpr/slice | solution.py:80
  134.3 2.5 %fusion.71 = f32[512,4,64]{0,2,1:T(8,128)S(1)} fusion(f32[4,512,1024]{2,1,0:T(8,128)S(1)} %get-tuple-element.231, f32[4,512]{1,0:T(4,128)S(1)} %add.173, f32[4,512]{1,0:T(4,128)S(1)} %max.13, pred[512,1024]{1,0:T(8,128)(4,1)S(1)} %fusion.66, bf16[1,4608,4,64]{1,3,2,0:T(8,128)(2,1)S(1)} %get-tuple-element.235, s32[]{:T(128)S(6)} %select_n.44), kind=kOutput, calls=%fused_computation.8.clone.1 | convolution fusion | flops 276824064 | bytes 9977860 | tf_op jit(solution)/shard_map/while/body/eval_jaxpr/hqk,khd->qhd/dot_general | solution.py:98
  139.8 2.8 %fusion.67 = (bf16[1,4608,4,64]{1,3,2,0:T(8,128)(2,1)S(1)}, bf16[1,4608,4,64]{1,3,2,0:T(8,128)(2,1)S(1)}) fusion(bf16[2,4608,4,64]{1,3,2,0:T(8,128)(2,1)} %get-tuple-element.262), kind=kLoop, calls=%fused_computation.71.clone.1 | loop fusion | bytes 9437184 | tf_op jit(solution)/shard_map/while/body/eval_jaxpr/slice | solution.py:80
  154.1 2.8 %fusion.67 = (bf16[1,4608,4,64]{1,3,2,0:T(8,128)(2,1)S(1)}, bf16[1,4608,4,64]{1,3,2,0:T(8,128)(2,1)S(1)}) fusion(bf16[2,4608,4,64]{1,3,2,0:T(8,128)(2,1)} %get-tuple-element.262), kind=kLoop, calls=%fused_computation.71.clone.1 | loop fusion | bytes 9437184 | tf_op jit(solution)/shard_map/while/body/eval_jaxpr/slice | solution.py:80
  163.0 2.5 %fusion.71 = f32[512,4,64]{0,2,1:T(8,128)S(1)} fusion(f32[4,512,1024]{2,1,0:T(8,128)S(1)} %get-tuple-element.231, f32[4,512]{1,0:T(4,128)S(1)} %add.173, f32[4,512]{1,0:T(4,128)S(1)} %max.13, pred[512,1024]{1,0:T(8,128)(4,1)S(1)} %fusion.66, bf16[1,4608,4,64]{1,3,2,0:T(8,128)(2,1)S(1)} %get-tuple-element.235, s32[]{:T(128)S(6)} %select_n.44), kind=kOutput, calls=%fused_computation.8.clone.1 | convolution fusion | flops 276824064 | bytes 9977860 | tf_op jit(solution)/shard_map/while/body/eval_jaxpr/hqk,khd->qhd/dot_general | solution.py:98
  168.5 2.8 %fusion.67 = (bf16[1,4608,4,64]{1,3,2,0:T(8,128)(2,1)S(1)}, bf16[1,4608,4,64]{1,3,2,0:T(8,128)(2,1)S(1)}) fusion(bf16[2,4608,4,64]{1,3,2,0:T(8,128)(2,1)} %get-tuple-element.262), kind=kLoop, calls=%fused_computation.71.clone.1 | loop fusion | bytes 9437184 | tf_op jit(solution)/shard_map/while/body/eval_jaxpr/slice | solution.py:80
  177.3 2.5 %fusion.71 = f32[512,4,64]{0,2,1:T(8,128)S(1)} fusion(f32[4,512,1024]{2,1,0:T(8,128)S(1)} %get-tuple-element.231, f32[4,512]{1,0:T(4,128)S(1)} %add.173, f32[4,512]{1,0:T(4,128)S(1)} %max.13, pred[512,1024]{1,0:T(8,128)(4,1)S(1)} %fusion.66, bf16[1,4608,4,64]{1,3,2,0:T(8,128)(2,1)S(1)} %get-tuple-element.235, s32[]{:T(128)S(6)} %select_n.44), kind=kOutput, calls=%fused_computation.8.clone.1 | convolution fusion | flops 276824064 | bytes 9977860 | tf_op jit(solution)/shard_map/while/body/eval_jaxpr/hqk,khd->qhd/dot_general | solution.py:98
  181.0 6.1 %fusion.36 = f32[4096,512]{1,0:T(8,128)} fusion(bf16[4096,256]{1,0:T(8,128)(2,1)} %bitcast.78, bf16[512,512]{1,0:T(8,128)(2,1)S(1)} %copy-done, s32[]{:T(128)S(6)} %select_n.23), kind=kOutput, calls=%fused_computation.56 | convolution fusion | flops 1073741824 | bytes 10747908 | tf_op jit(solution)/shard_map/dot_general | solution.py:111
  187.0 17.7 %reduce-scatter.2.cloned.1.call-done = f32[4096,256]{1,0:T(8,128)} async-done(((f32[4096,512]{1,0:T(8,128)}), f32[4096,256]{1,0:T(8,128)}) %reduce-scatter.2.cloned.1.call-update) | async-done | bytes 4194320 | tf_op jit(solution)/shard_map/reduce_scatter | solution.py:112
  204.7 3.7 %convert_element_type.64 = bf16[4096,256]{1,0:T(8,128)(2,1)} convert(f32[4096,256]{1,0:T(8,128)} %reduce-scatter.2.cloned.1.call-done) | non-fusion elementwise | flops 1048576 | bytes 6291456 | tf_op jit(solution)/shard_map/convert_element_type | solution.py:113
  (149 shorter events, 79.5 us)
Async XLA Ops:
  6.5 174.4 %copy-start = (bf16[512,512]{1,0:T(8,128)(2,1)S(1)}, bf16[512,512]{1,0:T(8,128)(2,1)}, u32[]{:S(2)}) copy-start(bf16[512,512]{1,0:T(8,128)(2,1)} %param.16) | copy-start | bytes 1572868
  6.5 3.3 %copy-start.6 = (f32[512]{0:T(512)S(1)}, f32[512]{0:T(512)}, u32[]{:S(2)}) copy-start(f32[512]{0:T(512)} %param.11) | copy-start | bytes 6148
  6.5 198.2 %reduce-scatter.2.cloned.1.call-start = ((), (), s32[]{:S(2)}) async-start(), calls=%async_computation.1 | async-start | bytes 12582912 | tf_op jit(solution)/shard_map/reduce_scatter | solution.py:112
  6.5 3.5 %copy-start.2 = (bf16[4096,512]{1,0:T(8,128)(2,1)S(1)}, bf16[4096,512]{1,0:T(8,128)(2,1)}, u32[]{:S(2)}) copy-start(bf16[4096,512]{1,0:T(8,128)(2,1)} %param.10) | copy-start | bytes 12582916
  10.1 1.1 copy-start.4
  11.2 10.5 %copy-start.1 = (bf16[4096,512]{1,0:T(8,128)(2,1)}, bf16[4096,512]{1,0:T(8,128)(2,1)S(1)}, u32[]{:S(2)}) copy-start(bf16[4096,512]{1,0:T(8,128)(2,1)S(1)} %fusion.32) | copy-start | bytes 12582916
  11.2 1.5 copy-start.7
  14.0 1.5 copy-start.3
  14.4 8.0 %copy-start.8 = (f32[512]{0:T(512)S(1)}, f32[512]{0:T(512)}, u32[]{:S(2)}) copy-start(f32[512]{0:T(512)} %param.12) | copy-start | bytes 6148
  14.4 8.5 %copy-start.5 = (bf16[512,256]{1,0:T(8,128)(2,1)S(1)}, bf16[512,256]{1,0:T(8,128)(2,1)}, u32[]{:S(2)}) copy-start(bf16[512,256]{1,0:T(8,128)(2,1)} %param.13) | copy-start | bytes 786436
  15.5 47.2 %collective-permute-start = (bf16[2,256,256]{1,2,0:T(8,128)(2,1)}, bf16[2,256,256]{1,2,0:T(8,128)(2,1)S(1)}, u32[]{:S(2)}, u32[]{:S(2)}) collective-permute-start(bf16[2,256,256]{1,2,0:T(8,128)(2,1)} %get-tuple-element.173), channel_id=1, source_target_pairs={{0,2},{2,4},{4,6},{6,8},{8,10},{10,12},{12,14},{1,3},{3,5},{5,7},{... | collective-permute-start | bytes 786440 | tf_op jit(solution)/shard_map/ppermute | solution.py:17
  20.4 42.4 %collective-permute-start.1 = (bf16[2,256,256]{1,2,0:T(8,128)(2,1)S(1)}, bf16[2,256,256]{1,2,0:T(8,128)(2,1)}, u32[]{:S(2)}, u32[]{:S(2)}) collective-permute-start(bf16[2,256,256]{1,2,0:T(8,128)(2,1)S(1)} %get-tuple-element.174), channel_id=1, source_target_pairs={{2,0},{4,2},{6,4},{8,6},{10,8},{12,10},{14,12},{3,1},{5,3},{7,5},{... | collective-permute-start | bytes 786440 | tf_op jit(solution)/shard_map/ppermute | solution.py:20
  22.9 3.6 %copy-start.9 = (f32[4]{0:T(128)S(1)}, f32[4]{0:T(128)}, u32[]{:S(2)}) copy-start(f32[4]{0:T(128)} %param.17) | copy-start | bytes 52
Sparse Core Ops, SparseCore 0:
  187.2 17.5 reduce-scatter.1
where the time goes:
time: 216 us; the launch traced here: 215 us
  matrix products  64.9 us (30%)
  other arithmetic  37.8 us (17%)
  local copies, waits for them, and re-layouts  36 us (17%)
  blocking collectives  32.9 us (15%)
  waiting for transfers between devices  17.7 us (8%)
  between operations  13.6 us (6%)
  starting transfers between devices  6.17 us (3%)
  loops' own time  6.09 us (3%)
    all_gather x1, blocking collectives, body(): coarse_all = lax.all_gather(coarse_stack, 'seq', axis=1, tiled=True)  32.9 us
    slice x8, local copies, waits for them, and re-layouts, one_block(): block_values = lax.dynamic_slice_in_dim(extended[1], row_start, span, 0)  22.7 us
    dot_general x8, matrix products, one_block(): jnp.einsum('hqk,khd->qhd', band_weights, block_values, preferred_element_...  20.1 us
    dot_general x8, matrix products, one_block(): jnp.einsum('qhd,khd->hqk', block_queries, block_keys, preferred_element_t...  19.9 us
    reduce_sum x8, other arithmetic, one_block(): jnp.sum(band_exp, axis=-1, keepdims=True)  18.2 us
    reduce_scatter x1, waiting for transfers between devices, body(): lax.psum_scatter(partial_out, 'head', scatter_dimension=1, tiled=True)  17.7 us
    dot_general x8, matrix products, one_block(): jnp.einsum('qhd,khd->hqk', block_queries, coarse_all[0], preferred_elemen...  9.05 us
    dynamic_update_slice x16, local copies, waits for them, and re-layouts, body(): lax.map(one_block, jnp.arange(tok_count // QB, dtype=jnp.int32))  6.92 us
  transfers between devices with their start and end apart: 3, of which 1 were waited for; matrix products, arithmetic and copies ran while one was open for 4% of the time, Pallas kernels for 0%

commit v1 on v0

--- a/solution.py
+++ b/solution.py
@@ -63,7 +63,24 @@
         jnp.bfloat16
     )
     coarse_stack = jnp.stack([coarse_keys.reshape(coarse.shape[0], width), coarse_values])
-    coarse_all = lax.all_gather(coarse_stack, "seq", axis=1, tiled=True)
+    size, here, rows = (lax.axis_size("seq"), lax.axis_index("seq"), coarse_stack.shape[1])
+    right = [(i_2, (i_2 + 1) % size) for i_2 in range(size)]
+    left = [(i_2, (i_2 - 1) % size) for i_2 in range(size)]
+    out = jnp.zeros(
+        (*coarse_stack.shape[:1], size * rows, *coarse_stack.shape[1 + 1 :]), coarse_stack.dtype
+    )
+    out = lax.dynamic_update_slice_in_dim(out, coarse_stack, here * rows, axis=1)
+    from_left = from_right = coarse_stack
+    half = size // 2
+    for lap in range(1, half + 1):
+        from_left = lax.ppermute(from_left, "seq", right)
+        out = lax.dynamic_update_slice_in_dim(out, from_left, (here - lap) % size * rows, axis=1)
+        if lap < size - half:
+            from_right = lax.ppermute(from_right, "seq", left)
+            out = lax.dynamic_update_slice_in_dim(
+                out, from_right, (here + lap) % size * rows, axis=1
+            )
+    coarse_all = out
     coarse_all = coarse_all.reshape(2, coarse_all.shape[1], local_heads, HEAD_DIM)
     span = QB + 2 * WINDOW
     offsets = (

time: 216 us -> 206 us (0.954)
  blocking collectives: 32.9 us -> 0 us
  starting transfers between devices: 6.17 us -> 19.4 us
  waiting for transfers between devices: 17.7 us -> 23.5 us
    all_gather x1 -> x0, blocking collectives: 32.9 us -> none  [body(): coarse_all = lax.all_gather(coarse_stack, 'seq', axis=1, tiled=True)]
    ppermute x0 -> x7, starting transfers between devices: none -> 16.8 us  [the longest x3 11.1 us: body(): from_right = lax.ppermute(from_right, 'seq', left)]
    ppermute x0 -> x7, waiting for transfers between devices: none -> 9.27 us  [the longest x4 9.26 us: body(): from_left = lax.ppermute(from_left, 'seq', right)]
    ppermute x1, starting transfers between devices: 4.87 us -> 1.29 us  [with_halo(): lax.ppermute(lax.slice_in_dim(block, block.shape[dim] - width, None, axis...]
    reduce_scatter x1, waiting for transfers between devices: 17.7 us -> 14.2 us  [body(): lax.psum_scatter(partial_out, 'head', scatter_dimension=1, tiled=True)]
    dot_general x1, matrix products: 1.41 us -> 3.6 us  [body(): jnp.dot(normed, w_key, preferred_element_type=jnp.float32)]
  transfers between devices with their start and end apart: 3 -> 10, of which waited for: 1 -> 4; matrix products, arithmetic and copies ran while one was open for 4% -> 6% of each run, Pallas kernels for 0% -> 0%
where the time goes in v1:
time: 206 us; the launch traced here: 205 us
  matrix products  66.2 us (32%)
  other arithmetic  38.3 us (19%)
  local copies, waits for them, and re-layouts  37.8 us (18%)
  waiting for transfers between devices  23.5 us (11%)
  starting transfers between devices  19.4 us (9%)
  between operations  13.7 us (7%)
  loops' own time  6.1 us (3%)
    slice x8, local copies, waits for them, and re-layouts, one_block(): block_values = lax.dynamic_slice_in_dim(extended[1], row_start, span, 0)  22.7 us
    dot_general x8, matrix products, one_block(): jnp.einsum('hqk,khd->qhd', band_weights, block_values, preferred_element_...  20.1 us
    dot_general x8, matrix products, one_block(): jnp.einsum('qhd,khd->hqk', block_queries, block_keys, preferred_element_t...  19.9 us
    reduce_sum x8, other arithmetic, one_block(): jnp.sum(band_exp, axis=-1, keepdims=True)  18.2 us
    reduce_scatter x1, waiting for transfers between devices, body(): lax.psum_scatter(partial_out, 'head', scatter_dimension=1, tiled=True)  14.2 us
    ppermute x3, starting transfers between devices, body(): from_right = lax.ppermute(from_right, 'seq', left)  11.1 us
    ppermute x4, waiting for transfers between devices, body(): from_left = lax.ppermute(from_left, 'seq', right)  9.26 us
    dot_general x8, matrix products, one_block(): jnp.einsum('qhd,khd->hqk', block_queries, coarse_all[0], preferred_elemen...  9.06 us
  transfers between devices with their start and end apart: 10, of which 4 were waited for; matrix products, arithmetic and copies ran while one was open for 6% of the time, Pallas kernels for 0%

profile of v1, /device:TPU:0, one launch (start us, length us, event | category | flops | bytes accessed | tf_op | source)
XLA Modules:
  0.0 205.0 jit_solution(9854560529704901598)
XLA Ops:
  6.5 3.2 %fusion.30 = f32[4096]{0:T(1024)S(1)} fusion(bf16[4096,512]{1,0:T(8,128)(2,1)} %param.10), kind=kLoop, calls=%fused_computation.40 | loop fusion | flops 6287360 | bytes 4210688 | tf_op jit(solution)/shard_map/reduce_sum | solution.py:26
  14.8 3.0 %collective-permute-start.2 = (bf16[2,4,256]{2,1,0:T(4,128)(2,1)S(1)}, bf16[2,4,256]{2,1,0:T(4,128)(2,1)S(1)}, u32[]{:S(2)}, u32[]{:S(2)}) collective-permute-start(bf16[2,4,256]{2,1,0:T(4,128)(2,1)S(1)} %get-tuple-element.161), channel_id=1, source_target_pairs={{0,2},{2,4},{4,6},{6,8},{8,10},{10,12},{12,14},{14,0},{1,3},{3,5},... | collective-permute-start | bytes 12296 | tf_op jit(solution)/shard_map/ppermute | solution.py:76
  17.9 3.1 %collective-permute-start.3 = (bf16[2,4,256]{2,1,0:T(4,128)(2,1)S(1)}, bf16[2,4,256]{2,1,0:T(4,128)(2,1)S(1)}, u32[]{:S(2)}, u32[]{:S(2)}) collective-permute-start(bf16[2,4,256]{2,1,0:T(4,128)(2,1)S(1)} %get-tuple-element.161), channel_id=1, source_target_pairs={{0,14},{2,0},{4,2},{6,4},{8,6},{10,8},{12,10},{14,12},{1,15},{3,1}... | collective-permute-start | bytes 12296 | tf_op jit(solution)/shard_map/ppermute | solution.py:79
  21.0 3.6 %bitcast_reduce_fusion = (f32[4096,4]{0,1:T(4,128)S(1)}, f32[4096,256]{0,1:T(8,128)S(1)}) fusion(bf16[4096,512]{1,0:T(8,128)(2,1)} %copy-done.1, bf16[512,256]{1,0:T(8,128)(2,1)S(1)} %copy-done.5), kind=kOutput, calls=%fused_computation.49 | convolution fusion | flops 1075822592 | bytes 8716288 | tf_op jit(solution)/shard_map/dot_general | solution.py:48
  30.1 3.5 %multiply_reduce_fusion = (f32[4096,4]{0,1:T(4,128)S(1)}, f32[4096,256]{0,1:T(8,128)S(1)}) fusion(bf16[4096,512]{1,0:T(8,128)(2,1)} %copy-done.1, bf16[512,256]{1,0:T(8,128)(2,1)S(1)} %copy-done.6), kind=kOutput, calls=%fused_computation.51 | convolution fusion | flops 1075822592 | bytes 8716288 | tf_op jit(solution)/shard_map/dot_general | solution.py:44
  35.6 2.6 %collective-permute-start.4 = (bf16[2,4,256]{2,1,0:T(4,128)(2,1)S(1)}, bf16[2,4,256]{2,1,0:T(4,128)(2,1)S(1)}, u32[]{:S(2)}, u32[]{:S(2)}) collective-permute-start(bf16[2,4,256]{2,1,0:T(4,128)(2,1)S(1)} %collective-permute-done.2), channel_id=1, source_target_pairs={{0,2},{2,4},{4,6},{6,8},{8,10},{10,12},{12,14},{14,0},{1,3},{3,5},... | collective-permute-start | bytes 12296 | tf_op jit(solution)/shard_map/ppermute | solution.py:76
  38.3 3.3 %collective-permute-start.5 = (bf16[2,4,256]{2,1,0:T(4,128)(2,1)S(1)}, bf16[2,4,256]{2,1,0:T(4,128)(2,1)S(1)}, u32[]{:S(2)}, u32[]{:S(2)}) collective-permute-start(bf16[2,4,256]{2,1,0:T(4,128)(2,1)S(1)} %collective-permute-done.3), channel_id=1, source_target_pairs={{0,14},{2,0},{4,2},{6,4},{8,6},{10,8},{12,10},{14,12},{1,15},{3,1}... | collective-permute-start | bytes 12296 | tf_op jit(solution)/shard_map/ppermute | solution.py:79
  43.1 4.8 %collective-permute-start.7 = (bf16[2,4,256]{2,1,0:T(4,128)(2,1)S(1)}, bf16[2,4,256]{2,1,0:T(4,128)(2,1)S(1)}, u32[]{:S(2)}, u32[]{:S(2)}) collective-permute-start(bf16[2,4,256]{2,1,0:T(4,128)(2,1)S(1)} %collective-permute-done.5), channel_id=1, source_target_pairs={{0,14},{2,0},{4,2},{6,4},{8,6},{10,8},{12,10},{14,12},{1,15},{3,1}... | collective-permute-start | bytes 12296 | tf_op jit(solution)/shard_map/ppermute | solution.py:79
  49.4 6.3 %collective-permute-done.8 = bf16[2,4,256]{2,1,0:T(4,128)(2,1)S(1)} collective-permute-done((bf16[2,4,256]{2,1,0:T(4,128)(2,1)S(1)}, bf16[2,4,256]{2,1,0:T(4,128)(2,1)S(1)}, u32[]{:S(2)}, u32[]{:S(2)}) %collective-permute-start.8) | collective-permute-done | bytes 4128 | tf_op jit(solution)/shard_map/ppermute | solution.py:76
  55.8 3.6 %pad_maximum_fusion = bf16[2,4608,256]{1,2,0:T(8,128)(2,1)} fusion(bf16[2,256,256]{1,2,0:T(8,128)(2,1)} %collective-permute-done.1, bf16[1,4096,256]{1,2,0:T(8,128)(2,1)} %copy-done.4, bf16[1,4096,256]{1,2,0:T(8,128)(2,1)S(1)} %bitcast.74, bf16[2,256,256]{1,2,0:T(8,128)(2,1)S(1)} %collective-permute-done), kind=kLoop, calls=%fused_computation.46 | loop fusion | flops 18874368 | bytes 9437184 | tf_op jit(solution)/shard_map/concatenate | solution.py:21
  59.5 114.6 %while.13 = (s32[]{:T(128)}, bf16[8,512,256]{2,1,0:T(8,128)(2,1)}, bf16[2,4608,4,64]{1,3,2,0:T(8,128)(2,1)}, s32[8]{0:T(128)S(1)}, s32[]{:T(128)}, /*index=5*/bf...) while((s32[]{:T(128)}, bf16[8,512,256]{2,1,0:T(8,128)(2,1)}, ...), condition=%wide.region_11.12_spmd.clone, body=%wide.region_6.11_spmd.clone.sunk | while | flops 575800320 | bytes 41618152 | solution.py:123
  61.3 2.8 %fusion.67 = (bf16[1,4608,4,64]{1,3,2,0:T(8,128)(2,1)S(1)}, bf16[1,4608,4,64]{1,3,2,0:T(8,128)(2,1)S(1)}) fusion(bf16[2,4608,4,64]{1,3,2,0:T(8,128)(2,1)} %get-tuple-element.250), kind=kLoop, calls=%fused_computation.79.clone.1 | loop fusion | bytes 9437184 | tf_op jit(solution)/shard_map/while/body/eval_jaxpr/slice | solution.py:97
  70.2 2.5 %fusion.71 = f32[512,4,64]{0,2,1:T(8,128)S(1)} fusion(f32[4,512,1024]{2,1,0:T(8,128)S(1)} %get-tuple-element.219, f32[4,512]{1,0:T(4,128)S(1)} %add.250, f32[4,512]{1,0:T(4,128)S(1)} %max.13, pred[512,1024]{1,0:T(8,128)(4,1)S(1)} %fusion.66, bf16[1,4608,4,64]{1,3,2,0:T(8,128)(2,1)S(1)} %get-tuple-element.223, s32[]{:T(128)S(6)} %select_n.114), kind=kOutput, calls=%fused_computation.8.clone.1 | convolution fusion | flops 276824064 | bytes 9977860 | tf_op jit(solution)/shard_map/while/body/eval_jaxpr/hqk,khd->qhd/dot_general | solution.py:115
  75.6 2.8 %fusion.67 = (bf16[1,4608,4,64]{1,3,2,0:T(8,128)(2,1)S(1)}, bf16[1,4608,4,64]{1,3,2,0:T(8,128)(2,1)S(1)}) fusion(bf16[2,4608,4,64]{1,3,2,0:T(8,128)(2,1)} %get-tuple-element.250), kind=kLoop, calls=%fused_computation.79.clone.1 | loop fusion | bytes 9437184 | tf_op jit(solution)/shard_map/while/body/eval_jaxpr/slice | solution.py:97
  90.0 2.8 %fusion.67 = (bf16[1,4608,4,64]{1,3,2,0:T(8,128)(2,1)S(1)}, bf16[1,4608,4,64]{1,3,2,0:T(8,128)(2,1)S(1)}) fusion(bf16[2,4608,4,64]{1,3,2,0:T(8,128)(2,1)} %get-tuple-element.250), kind=kLoop, calls=%fused_computation.79.clone.1 | loop fusion | bytes 9437184 | tf_op jit(solution)/shard_map/while/body/eval_jaxpr/slice | solution.py:97
  104.3 2.8 %fusion.67 = (bf16[1,4608,4,64]{1,3,2,0:T(8,128)(2,1)S(1)}, bf16[1,4608,4,64]{1,3,2,0:T(8,128)(2,1)S(1)}) fusion(bf16[2,4608,4,64]{1,3,2,0:T(8,128)(2,1)} %get-tuple-element.250), kind=kLoop, calls=%fused_computation.79.clone.1 | loop fusion | bytes 9437184 | tf_op jit(solution)/shard_map/while/body/eval_jaxpr/slice | solution.py:97
  113.1 2.5 %fusion.71 = f32[512,4,64]{0,2,1:T(8,128)S(1)} fusion(f32[4,512,1024]{2,1,0:T(8,128)S(1)} %get-tuple-element.219, f32[4,512]{1,0:T(4,128)S(1)} %add.250, f32[4,512]{1,0:T(4,128)S(1)} %max.13, pred[512,1024]{1,0:T(8,128)(4,1)S(1)} %fusion.66, bf16[1,4608,4,64]{1,3,2,0:T(8,128)(2,1)S(1)} %get-tuple-element.223, s32[]{:T(128)S(6)} %select_n.114), kind=kOutput, calls=%fused_computation.8.clone.1 | convolution fusion | flops 276824064 | bytes 9977860 | tf_op jit(solution)/shard_map/while/body/eval_jaxpr/hqk,khd->qhd/dot_general | solution.py:115
  118.6 2.8 %fusion.67 = (bf16[1,4608,4,64]{1,3,2,0:T(8,128)(2,1)S(1)}, bf16[1,4608,4,64]{1,3,2,0:T(8,128)(2,1)S(1)}) fusion(bf16[2,4608,4,64]{1,3,2,0:T(8,128)(2,1)} %get-tuple-element.250), kind=kLoop, calls=%fused_computation.79.clone.1 | loop fusion | bytes 9437184 | tf_op jit(solution)/shard_map/while/body/eval_jaxpr/slice | solution.py:97
  132.9 2.8 %fusion.67 = (bf16[1,4608,4,64]{1,3,2,0:T(8,128)(2,1)S(1)}, bf16[1,4608,4,64]{1,3,2,0:T(8,128)(2,1)S(1)}) fusion(bf16[2,4608,4,64]{1,3,2,0:T(8,128)(2,1)} %get-tuple-element.250), kind=kLoop, calls=%fused_computation.79.clone.1 | loop fusion | bytes 9437184 | tf_op jit(solution)/shard_map/while/body/eval_jaxpr/slice | solution.py:97
  147.3 2.8 %fusion.67 = (bf16[1,4608,4,64]{1,3,2,0:T(8,128)(2,1)S(1)}, bf16[1,4608,4,64]{1,3,2,0:T(8,128)(2,1)S(1)}) fusion(bf16[2,4608,4,64]{1,3,2,0:T(8,128)(2,1)} %get-tuple-element.250), kind=kLoop, calls=%fused_computation.79.clone.1 | loop fusion | bytes 9437184 | tf_op jit(solution)/shard_map/while/body/eval_jaxpr/slice | solution.py:97
  161.6 2.8 %fusion.67 = (bf16[1,4608,4,64]{1,3,2,0:T(8,128)(2,1)S(1)}, bf16[1,4608,4,64]{1,3,2,0:T(8,128)(2,1)S(1)}) fusion(bf16[2,4608,4,64]{1,3,2,0:T(8,128)(2,1)} %get-tuple-element.250), kind=kLoop, calls=%fused_computation.79.clone.1 | loop fusion | bytes 9437184 | tf_op jit(solution)/shard_map/while/body/eval_jaxpr/slice | solution.py:97
  174.1 6.1 %fusion.36 = f32[4096,512]{1,0:T(8,128)} fusion(bf16[4096,256]{1,0:T(8,128)(2,1)} %bitcast.76, bf16[512,512]{1,0:T(8,128)(2,1)S(1)} %copy-done, s32[]{:T(128)S(6)} %select_n.93), kind=kOutput, calls=%fused_computation.56 | convolution fusion | flops 1073741824 | bytes 10747908 | tf_op jit(solution)/shard_map/dot_general | solution.py:128
  180.2 14.2 %reduce-scatter.2.cloned.1.call-done = f32[4096,256]{1,0:T(8,128)} async-done(((f32[4096,512]{1,0:T(8,128)}), f32[4096,256]{1,0:T(8,128)}) %reduce-scatter.2.cloned.1.call-update) | async-done | bytes 4194320 | tf_op jit(solution)/shard_map/reduce_scatter | solution.py:129
  194.4 3.7 %convert_element_type.64 = bf16[4096,256]{1,0:T(8,128)(2,1)} convert(f32[4096,256]{1,0:T(8,128)} %reduce-scatter.2.cloned.1.call-done) | non-fusion elementwise | flops 1048576 | bytes 6291456 | tf_op jit(solution)/shard_map/convert_element_type | solution.py:130
  (171 shorter events, 96.3 us)
Async XLA Ops:
  6.5 167.6 %copy-start = (bf16[512,512]{1,0:T(8,128)(2,1)S(1)}, bf16[512,512]{1,0:T(8,128)(2,1)}, u32[]{:S(2)}) copy-start(bf16[512,512]{1,0:T(8,128)(2,1)} %param.16) | copy-start | bytes 1572868
  6.5 3.3 %copy-start.7 = (f32[512]{0:T(512)S(1)}, f32[512]{0:T(512)}, u32[]{:S(2)}) copy-start(f32[512]{0:T(512)} %param.11) | copy-start | bytes 6148
  6.5 187.9 %reduce-scatter.2.cloned.1.call-start = ((), (), s32[]{:S(2)}) async-start(), calls=%async_computation.1 | async-start | bytes 12582912 | tf_op jit(solution)/shard_map/reduce_scatter | solution.py:129
  6.5 3.5 %copy-start.3 = (bf16[4096,512]{1,0:T(8,128)(2,1)S(1)}, bf16[4096,512]{1,0:T(8,128)(2,1)}, u32[]{:S(2)}) copy-start(bf16[4096,512]{1,0:T(8,128)(2,1)} %param.10) | copy-start | bytes 12582916
  11.2 1.9 copy-start.1
  13.1 0.9 copy-start.5
  13.1 1.0 copy-start.9
  13.1 1.5 copy-start.8
  14.8 9.7 %copy-start.2 = (bf16[4096,512]{1,0:T(8,128)(2,1)S(1)}, bf16[4096,512]{1,0:T(8,128)(2,1)}, u32[]{:S(2)}) copy-start(bf16[4096,512]{1,0:T(8,128)(2,1)} %copy-done.1) | copy-start | bytes 12582916
  14.8 20.8 %collective-permute-start.2 = (bf16[2,4,256]{2,1,0:T(4,128)(2,1)S(1)}, bf16[2,4,256]{2,1,0:T(4,128)(2,1)S(1)}, u32[]{:S(2)}, u32[]{:S(2)}) collective-permute-start(bf16[2,4,256]{2,1,0:T(4,128)(2,1)S(1)} %get-tuple-element.161), channel_id=1, source_target_pairs={{0,2},{2,4},{4,6},{6,8},{8,10},{10,12},{12,14},{14,0},{1,3},{3,5},... | collective-permute-start | bytes 12296 | tf_op jit(solution)/shard_map/ppermute | solution.py:76
  17.9 20.4 %collective-permute-start.3 = (bf16[2,4,256]{2,1,0:T(4,128)(2,1)S(1)}, bf16[2,4,256]{2,1,0:T(4,128)(2,1)S(1)}, u32[]{:S(2)}, u32[]{:S(2)}) collective-permute-start(bf16[2,4,256]{2,1,0:T(4,128)(2,1)S(1)} %get-tuple-element.161), channel_id=1, source_target_pairs={{0,14},{2,0},{4,2},{6,4},{8,6},{10,8},{12,10},{14,12},{1,15},{3,1}... | collective-permute-start | bytes 12296 | tf_op jit(solution)/shard_map/ppermute | solution.py:79
  25.9 1.5 copy-start.4
  26.0 4.1 %copy-start.6 = (bf16[512,256]{1,0:T(8,128)(2,1)S(1)}, bf16[512,256]{1,0:T(8,128)(2,1)}, u32[]{:S(2)}) copy-start(bf16[512,256]{1,0:T(8,128)(2,1)} %param.13) | copy-start | bytes 786436
  27.4 28.4 %collective-permute-start = (bf16[2,256,256]{1,2,0:T(8,128)(2,1)}, bf16[2,256,256]{1,2,0:T(8,128)(2,1)S(1)}, u32[]{:S(2)}, u32[]{:S(2)}) collective-permute-start(bf16[2,256,256]{1,2,0:T(8,128)(2,1)} %get-tuple-element.159), channel_id=1, source_target_pairs={{0,2},{2,4},{4,6},{6,8},{8,10},{10,12},{12,14},{1,3},{3,5},{5,7},{... | collective-permute-start | bytes 786440 | tf_op jit(solution)/shard_map/ppermute | solution.py:17
  28.7 27.1 %collective-permute-start.1 = (bf16[2,256,256]{1,2,0:T(8,128)(2,1)S(1)}, bf16[2,256,256]{1,2,0:T(8,128)(2,1)}, u32[]{:S(2)}, u32[]{:S(2)}) collective-permute-start(bf16[2,256,256]{1,2,0:T(8,128)(2,1)S(1)} %get-tuple-element.160), channel_id=1, source_target_pairs={{2,0},{4,2},{6,4},{8,6},{10,8},{12,10},{14,12},{3,1},{5,3},{7,5},{... | collective-permute-start | bytes 786440 | tf_op jit(solution)/shard_map/ppermute | solution.py:20
  30.1 3.6 %copy-start.10 = (f32[4]{0:T(128)S(1)}, f32[4]{0:T(128)}, u32[]{:S(2)}) copy-start(f32[4]{0:T(128)} %param.17) | copy-start | bytes 52
  35.6 7.4 %collective-permute-start.4 = (bf16[2,4,256]{2,1,0:T(4,128)(2,1)S(1)}, bf16[2,4,256]{2,1,0:T(4,128)(2,1)S(1)}, u32[]{:S(2)}, u32[]{:S(2)}) collective-permute-start(bf16[2,4,256]{2,1,0:T(4,128)(2,1)S(1)} %collective-permute-done.2), channel_id=1, source_target_pairs={{0,2},{2,4},{4,6},{6,8},{8,10},{10,12},{12,14},{14,0},{1,3},{3,5},... | collective-permute-start | bytes 12296 | tf_op jit(solution)/shard_map/ppermute | solution.py:76
  38.3 4.8 %collective-permute-start.5 = (bf16[2,4,256]{2,1,0:T(4,128)(2,1)S(1)}, bf16[2,4,256]{2,1,0:T(4,128)(2,1)S(1)}, u32[]{:S(2)}, u32[]{:S(2)}) collective-permute-start(bf16[2,4,256]{2,1,0:T(4,128)(2,1)S(1)} %collective-permute-done.3), channel_id=1, source_target_pairs={{0,14},{2,0},{4,2},{6,4},{8,6},{10,8},{12,10},{14,12},{1,15},{3,1}... | collective-permute-start | bytes 12296 | tf_op jit(solution)/shard_map/ppermute | solution.py:79
  43.1 6.3 %collective-permute-start.6 = (bf16[2,4,256]{2,1,0:T(4,128)(2,1)S(1)}, bf16[2,4,256]{2,1,0:T(4,128)(2,1)S(1)}, u32[]{:S(2)}, u32[]{:S(2)}) collective-permute-start(bf16[2,4,256]{2,1,0:T(4,128)(2,1)S(1)} %collective-permute-done.4), channel_id=1, source_target_pairs={{0,2},{2,4},{4,6},{6,8},{8,10},{10,12},{12,14},{14,0},{1,3},{3,5},... | collective-permute-start | bytes 12296 | tf_op jit(solution)/shard_map/ppermute | solution.py:76
  43.1 6.3 %collective-permute-start.7 = (bf16[2,4,256]{2,1,0:T(4,128)(2,1)S(1)}, bf16[2,4,256]{2,1,0:T(4,128)(2,1)S(1)}, u32[]{:S(2)}, u32[]{:S(2)}) collective-permute-start(bf16[2,4,256]{2,1,0:T(4,128)(2,1)S(1)} %collective-permute-done.5), channel_id=1, source_target_pairs={{0,14},{2,0},{4,2},{6,4},{8,6},{10,8},{12,10},{14,12},{1,15},{3,1}... | collective-permute-start | bytes 12296 | tf_op jit(solution)/shard_map/ppermute | solution.py:79
  49.4 6.3 %collective-permute-start.8 = (bf16[2,4,256]{2,1,0:T(4,128)(2,1)S(1)}, bf16[2,4,256]{2,1,0:T(4,128)(2,1)S(1)}, u32[]{:S(2)}, u32[]{:S(2)}) collective-permute-start(bf16[2,4,256]{2,1,0:T(4,128)(2,1)S(1)} %collective-permute-done.6), channel_id=1, source_target_pairs={{0,2},{2,4},{4,6},{6,8},{8,10},{10,12},{12,14},{14,0},{1,3},{3,5},... | collective-permute-start | bytes 12296 | tf_op jit(solution)/shard_map/ppermute | solution.py:76
Sparse Core Ops, SparseCore 0:
  180.3 14.0 reduce-scatter.1
